TPU v7x, 256 devices: a whole 4x4x8 slice. The times are simulated.
256 devices in a mesh: space: 32 (over y_hi, z, core), coil: 8 (over y_lo, x).
Axes of the slice: x: 4, y: 4 (y_hi: 2, y_lo: 2; y = y_hi * 2 + y_lo), z: 8, core: 2. Of those that a mesh axis runs over, the one named last changes fastest.
Arguments:
- spatial_coef: bfloat16 [16, 128, 128, 2, 128], P('coil', 'space'), may hold values from -6 to 6
- temporal_basis: bfloat16 [2, 16, 4], replicated, may hold values from -1.5 to 1.5
- coil_maps: bfloat16 [32, 128, 128, 2, 128], P('coil', 'space'), may hold values from -6 to 6
- field_steps: int32 [128, 128, 128], P('space'), may hold values from 0 to 255
- kspace_data: bfloat16 [32, 4, 128, 128, 2, 128], P('coil', None, None, 'space'), may hold values from -6 to 6
- sample_mask: int32 [4, 128, 128], P(None, 'space'), may hold values 0 or 1
Outputs:
- gradient: float32 [16, 128, 128, 2, 128], P('coil', 'space')
Inputs may be any that keep to these rules, and one draw needn't show every extreme that they name: `sample_mask`: 1 where a phase-encoding line is sampled at that point, else 0.
All inputs are finite; a program needn't handle non-finite values. No bound on the sum of `sample_mask` on one device may be relied on, other than what follows from the above.
Results may differ from a plain program's by a relative error of at most 0.014.
Values may be sent and summed in bfloat16 or wider, within the bound.
A program may use at most 64 MiB of HBM per device.

v0:
```python
import math
import jax
import jax.numpy as jnp
from jax import lax
from jax.sharding import PartitionSpec as P

STEPS_CYCLE = 256


def dft_table(length, sign):
    index = jnp.arange(length, dtype=jnp.int32)
    steps = index[:, None] * index[None, :] % length
    angle = steps.astype(jnp.float32) * (2.0 * math.pi / length)
    scale = 1.0 / math.sqrt(length)
    cosine = jnp.cos(angle) * scale
    sine = jnp.sin(angle) * (sign * scale)
    upper = jnp.stack([cosine, sine], axis=1)
    lower = jnp.stack([-sine, cosine], axis=1)
    return jnp.stack([upper, lower], axis=0).astype(jnp.bfloat16)


def forward_mix(basis):
    real_part = basis[0]
    imaginary = basis[1]
    return jnp.stack(
        [jnp.stack([real_part, imaginary], -1), jnp.stack([-imaginary, real_part], -1)], 1
    )


def adjoint_mix(basis):
    real_part = basis[0].T
    imaginary = basis[1].T
    return jnp.stack(
        [jnp.stack([real_part, -imaginary], -1), jnp.stack([imaginary, real_part], -1)], 1
    )


def phase_parts(field_steps, points):
    counter = jnp.arange(1, points + 1, dtype=jnp.int32)
    steps = field_steps[None] * counter[:, None, None, None] % STEPS_CYCLE
    angle = steps.astype(jnp.float32) * (2.0 * math.pi / STEPS_CYCLE)
    return (jnp.cos(angle), jnp.sin(angle))


def transform(volume, table, form):
    return jnp.einsum(form, volume, table, preferred_element_type=jnp.float32)


def shards(spatial_coef, temporal_basis, coil_maps, field_steps, kspace_data, sample_mask):
    points = temporal_basis.shape[2]
    section = temporal_basis
    image = jnp.einsum(
        "lxypz,lptq->txyqz",
        lax.all_gather(spatial_coef, "coil", axis=0, tiled=True),
        forward_mix(section),
        preferred_element_type=jnp.float32,
    )
    cosine, sine = phase_parts(field_steps, points)
    image_real = image[:, :, :, 0]
    image_imaginary = image[:, :, :, 1]
    turned_real = cosine * image_real - sine * image_imaginary
    turned_imaginary = sine * image_real + cosine * image_imaginary
    map_real = coil_maps[:, :, :, 0].astype(jnp.float32)[:, None]
    map_imaginary = coil_maps[:, :, :, 1].astype(jnp.float32)[:, None]
    coil_real = map_real * turned_real - map_imaginary * turned_imaginary
    coil_imaginary = map_real * turned_imaginary + map_imaginary * turned_real
    coil_image = jnp.stack([coil_real, coil_imaginary], axis=4).astype(jnp.bfloat16)
    depth_count = coil_image.shape[5]
    row_count = coil_image.shape[3]
    depth_pass = transform(coil_image, dft_table(depth_count, -1.0), "ctxypz,pzqk->ctxyqk").astype(
        jnp.bfloat16
    )
    row_pass = transform(depth_pass, dft_table(row_count, -1.0), "ctxypz,pyqk->ctxkqz").astype(
        jnp.bfloat16
    )
    slabs = lax.all_to_all(row_pass, "space", split_axis=3, concat_axis=2, tiled=True)
    first_count = slabs.shape[2]
    kspace = transform(slabs, dft_table(first_count, -1.0), "ctxypz,pxqk->ctkyqz")
    mask_float = sample_mask.astype(jnp.float32)[None, :, None, :, None, :]
    residual = (mask_float * (kspace - kspace_data.astype(jnp.float32))).astype(jnp.bfloat16)
    back_first = transform(residual, dft_table(first_count, 1.0), "ctxypz,pxqk->ctkyqz").astype(
        jnp.bfloat16
    )
    returned = lax.all_to_all(back_first, "space", split_axis=2, concat_axis=3, tiled=True)
    back_rows = transform(returned, dft_table(row_count, 1.0), "ctxypz,pyqk->ctxkqz").astype(
        jnp.bfloat16
    )
    back_image = transform(back_rows, dft_table(depth_count, 1.0), "ctxypz,pzqk->ctxyqk")
    back_real = back_image[:, :, :, :, 0]
    back_imaginary = back_image[:, :, :, :, 1]
    sum_real = jnp.sum(map_real * back_real + map_imaginary * back_imaginary, axis=0)
    sum_imaginary = jnp.sum(map_real * back_imaginary - map_imaginary * back_real, axis=0)
    combined_real = cosine * sum_real + sine * sum_imaginary
    combined_imaginary = cosine * sum_imaginary - sine * sum_real
    combined = jnp.stack([combined_real, combined_imaginary], axis=3)
    section = temporal_basis.astype(jnp.float32)
    return lax.psum_scatter(
        jnp.einsum(
            "txypz,tplq->lxyqz", combined, adjoint_mix(section), precision=lax.Precision.HIGHEST
        ).astype(jnp.bfloat16),
        "coil",
        scatter_dimension=0,
        tiled=True,
    ).astype(jnp.float32)


def solution(mesh):
    in_specs = (
        P("coil", "space", None, None, None),
        P(),
        P("coil", "space", None, None, None),
        P("space", None, None),
        P("coil", None, None, "space", None, None),
        P(None, "space", None),
    )
    out_specs = P("coil", "space", None, None, None)
    return jax.shard_map(shards, mesh=mesh, in_specs=in_specs, out_specs=out_specs, check_vma=False)
```

profile of v0, /device:TPU:1, one launch (start us, length us, event | category | flops | bytes accessed | tf_op | source)
XLA Modules:
  0.0 418.4 jit_solution(10272380356210166558)
XLA Ops:
  6.5 0.0 all-gather.2.cloned.1.call-start
  6.5 1.9 copy.65
  8.5 0.0 all-gather.2.cloned.1.call-update
  8.5 0.7 fusion.72
  9.2 0.7 slice_bitcast_fusion.6
  9.9 0.3 multiply_convert_fusion.2
  10.2 0.3 negate_convert_fusion
  10.5 0.3 multiply_convert_fusion
  10.8 3.6 slice_convert_fusion.1
  14.4 53.7 %all-gather.2.cloned.1.call-done = bf16[16,4,128,2,128]{4,2,3,1,0:T(8,128)(2,1)} async-done(((bf16[2,4,128,2,128]{4,2,3,1,0:T(8,128)(2,1)}), bf16[16,4,128,2,128]{4,2,3,1,0:T(8,128)(2,1)}) %all-gather.2.cloned.1.call-update) | async-done | bytes 4194320 | tf_op jit(solution)/shard_map/all_gather | solution.py:54
  68.1 0.0 copy-start.1
  68.1 4.9 %fusion.31 = f32[4,2,4,128,128]{4,0,3,2,1:T(4,128)S(1)} fusion(bf16[16,4,128,2,128]{4,2,3,1,0:T(8,128)(2,1)} %all-gather.2.cloned.1.call-done, bf16[16,1,4,2]{0,2,1,3:T(4,128)(2,1)S(1)} %get-tuple-element.26, bf16[16,1,4,2]{0,2,1,3:T(4,128)(2,1)S(1)} %get-tuple-element.25), kind=kOutput, calls=%fused_computation.43 | convolution fusion | flops 33555456 | bytes 6291968 | tf_op jit(solution)/shard_map/lxypz,lptq->txyqz/dot_general | solution.py:52
  73.0 0.3 copy.134
  73.2 0.0 copy-done.1
  73.2 4.6 %multiply_subtract_fusion = (f32[4,4,128,128]{3,2,1,0:T(8,128)S(1)}, f32[4,4,128,128]{3,2,1,0:T(8,128)S(1)}) fusion(f32[4,4,128,2,128]{4,2,1,0,3:T(8,128)S(1)} %bitcast.244, s32[4]{0:T(128)S(1)} %iota_add_fusion, s32[4,128,128]{2,1,0:T(8,128)S(1)} %copy-done.1), kind=kLoop, calls=%fused_computation.64 | loop fusion | flops 5242880 | bytes 4456464 | tf_op jit(solution)/shard_map/sub | solution.py:61
  77.9 3.1 subtract_convert_fusion
  81.0 6.7 %fusion.5 = bf16[4,4,4,128,2,128]{5,3,2,1,0,4:T(8,128)(2,1)} fusion(bf16[4,4,4,128,1,128]{5,3,4,2,1,0:T(8,128)(2,1)} %get-tuple-element.8, bf16[4,4,4,128,1,128]{5,3,4,2,1,0:T(8,128)(2,1)} %get-tuple-element.7, bf16[1,128,2,128]{3,1,0,2:T(8,128)(2,1)S(1)} %get-tuple-element.16, bf16[1,128,2,128]{3,1,0,2:T(8,128)(2,1)S(1)} %get-tuple-element.17), kind=kOutput, calls=%fused_computation.10 | convolution fusion | flops 2160590848 | bytes 8519680 | tf_op jit(solution)/shard_map/ctxypz,pyqk->ctxkqz/dot_general | solution.py:46
  87.7 7.4 %copy.69 = bf16[4,4,4,128,2,128]{5,2,1,0,4,3:T(4,128)(2,1)} copy(bf16[4,4,4,128,2,128]{5,3,2,1,0,4:T(8,128)(2,1)} %fusion.5) | data formatting | bytes 8388608 | tf_op jit(solution)/shard_map/convert_element_type | solution.py:73
  95.1 0.0 copy-start.3
  95.1 10.2 %all-to-all-start = ((bf16[4,4,4,128,2,128]{5,2,1,0,4,3:T(4,128)(2,1)}), bf16[4,4,4,128,2,128]{5,2,1,0,4,3:T(4,128)(2,1)}, u32[]{:S(2)}, u32[]{:S(2)}) async-start(bf16[4,4,4,128,2,128]{5,2,1,0,4,3:T(4,128)(2,1)} %copy.69), calls=%async_computation | async-start | bytes 8388608 | tf_op jit(solution)/shard_map/all_to_all | solution.py:76
  105.3 0.0 copy-done.3
  105.3 96.1 %all-to-all-done = bf16[4,4,4,128,2,128]{5,2,1,0,4,3:T(4,128)(2,1)} async-done(((bf16[4,4,4,128,2,128]{5,2,1,0,4,3:T(4,128)(2,1)}), bf16[4,4,4,128,2,128]{5,2,1,0,4,3:T(4,128)(2,1)}, u32[]{:S(2)}, u32[]{:S(2)}) %all-to-all-start) | async-done | bytes 4194336 | tf_op jit(solution)/shard_map/all_to_all | solution.py:76
  201.5 0.0 copy-start
  201.5 4.7 %copy.70 = bf16[4,4,4,32,4,2,128]{6,2,3,5,4,1,0:T(4,128)(2,1)S(1)} copy(bf16[4,4,4,32,4,2,128]{6,2,1,0,5,4,3:T(4,128)(2,1)} %bitcast.51) | data formatting | bytes 8388608 | tf_op jit(solution)/shard_map/all_to_all | solution.py:76
  206.2 0.0 copy-done
  206.2 1.4 fusion.1
  207.6 1.3 fusion.6
  208.8 5.2 %copy.75 = bf16[4,4,128,4,2,128]{5,3,1,0,4,2:T(4,128)(2,1)} copy(bf16[4,4,128,4,2,128]{5,2,3,1,0,4:T(8,128)(2,1)S(1)} %fusion.6) | data formatting | bytes 8388608 | tf_op jit(solution)/shard_map/convert_element_type | solution.py:81
  214.1 0.0 copy-start.2
  214.1 7.4 %all-to-all-start.1 = ((bf16[4,4,128,4,2,128]{5,3,1,0,4,2:T(4,128)(2,1)}), bf16[4,4,128,4,2,128]{5,3,1,0,4,2:T(4,128)(2,1)}, u32[]{:S(2)}, u32[]{:S(2)}) async-start(bf16[4,4,128,4,2,128]{5,3,1,0,4,2:T(4,128)(2,1)} %copy.75), calls=%async_computation.1 | async-start | bytes 8388608 | tf_op jit(solution)/shard_map/all_to_all | solution.py:84
  221.5 0.0 reduce-scatter.2.cloned.1.call-start
  221.5 0.0 copy-done.2
  221.6 96.1 %all-to-all-done.1 = bf16[4,4,128,4,2,128]{5,3,1,0,4,2:T(4,128)(2,1)} async-done(((bf16[4,4,128,4,2,128]{5,3,1,0,4,2:T(4,128)(2,1)}), bf16[4,4,128,4,2,128]{5,3,1,0,4,2:T(4,128)(2,1)}, u32[]{:S(2)}, u32[]{:S(2)}) %all-to-all-start.1) | async-done | bytes 4194336 | tf_op jit(solution)/shard_map/all_to_all | solution.py:84
  317.7 6.5 %copy.76 = bf16[4,4,32,4,4,2,128]{6,4,2,5,3,1,0:T(4,128)(2,1)} copy(bf16[4,4,32,4,4,2,128]{6,4,1,0,5,3,2:T(4,128)(2,1)} %bitcast.62) | data formatting | bytes 8388608 | tf_op jit(solution)/shard_map/all_to_all | solution.py:84
  324.2 7.8 %fusion.20 = f32[4,4,4,128,2,128]{5,3,4,2,1,0:T(8,128)} fusion(bf16[4,4,4,128,2,128,1]{5,3,6,4,2,1,0:T(8,128)(2,1)} %bitcast.238, bf16[1,128,2,128]{3,1,2,0:T(8,128)(2,1)S(1)} %get-tuple-element.18, bf16[1,128,2,128]{3,1,2,0:T(8,128)(2,1)S(1)} %get-tuple-element.15), kind=kOutput, calls=%fused_computation.31 | convolution fusion | flops 2150105088 | bytes 12713984 | tf_op jit(solution)/shard_map/ctxypz,pzqk->ctxyqk/dot_general | solution.py:46
  332.0 4.6 %add_reduce_fusion = (f32[4,4,128,128]{3,2,1,0:T(8,128)S(1)}, f32[4,4,128,128]{3,2,1,0:T(8,128)S(1)}) fusion(f32[4,4,4,128,2,128]{5,3,4,2,1,0:T(8,128)} %fusion.20, f32[4,4,128,128]{3,2,1,0:T(8,128)S(1)} %bitcast.243, f32[4,4,128,128]{3,2,1,0:T(8,128)S(1)} %bitcast.241), kind=kLoop, calls=%fused_computation.28 | loop fusion | flops 7864320 | bytes 12582912 | tf_op jit(solution)/shard_map/reduce_sum | solution.py:91
  336.6 9.6 %fusion.40 = (f32[4,4,128,1,128]{4,0,3,2,1:T(4,128)S(1)}, f32[4,4,128,1,128]{4,0,3,2,1:T(4,128)S(1)}) fusion(f32[4,4,128,128]{3,2,1,0:T(8,128)S(1)} %get-tuple-element.6, f32[4,4,128,128]{3,2,1,0:T(8,128)S(1)} %get-tuple-element.5, s32[4]{0:T(128)S(1)} %iota_add_fusion, s32[4,128,128]{2,1,0:T(8,128)S(1)} %copy-done.1), kind=kLoop, calls=%fused_computation.58 | loop fusion | flops 5242880 | bytes 4456464 | tf_op jit(solution)/shard_map/add | solution.py:93
  346.2 7.8 %fusion.7 = bf16[16,4,128,2,128]{4,0,2,1,3:T(8,128)(2,1)S(1)} fusion(f32[4,4,128,1,128]{4,0,3,2,1:T(4,128)S(1)} %get-tuple-element.10, f32[4,4,128,1,128]{4,0,3,2,1:T(4,128)S(1)} %get-tuple-element.9, f32[4,1,16,2]{2,0,1,3:T(4,128)S(1)} %get-tuple-element.22, f32[4,1,16,2]{2,0,1,3:T(4,128)S(1)} %get-tuple-element.21), kind=kOutput, calls=%fused_computation.12 | convolution fusion | flops 203948288 | bytes 6292480 | tf_op jit(solution)/shard_map/txypz,tplq->lxyqz/dot_general | solution.py:98
  354.0 3.1 copy.82
  357.1 0.0 reduce-scatter.2.cloned.1.call-update
  357.1 51.9 %reduce-scatter.2.cloned.1.call-done = bf16[2,4,128,2,128]{4,2,3,1,0:T(8,128)(2,1)} async-done(((bf16[16,4,128,2,128]{4,2,3,1,0:T(8,128)(2,1)}), bf16[2,4,128,2,128]{4,2,3,1,0:T(8,128)(2,1)}) %reduce-scatter.2.cloned.1.call-update) | async-done | bytes 524304 | tf_op jit(solution)/shard_map/reduce_scatter | solution.py:97
  409.0 2.6 copy.83
  (8 shorter events, 0.1 us)
Async XLA Ops:
  6.5 61.6 %all-gather.2.cloned.1.call-start = ((), (), s32[]{:S(2)}) async-start(), calls=%async_computation.3 | async-start | bytes 4718592 | tf_op jit(solution)/shard_map/all_gather | solution.py:54
  68.1 5.1 %copy-start.1 = (s32[4,128,128]{2,1,0:T(8,128)S(1)}, s32[4,128,128]{2,1,0:T(8,128)}, u32[]{:S(2)}) copy-start(s32[4,128,128]{2,1,0:T(8,128)} %param.9) | copy-start | bytes 786436
  95.1 10.2 %copy-start.3 = (s32[4,4,128]{2,1,0:T(4,128)S(1)}, s32[4,4,128]{2,1,0:T(4,128)}, u32[]{:S(2)}) copy-start(s32[4,4,128]{2,1,0:T(4,128)} %param.11) | copy-start | bytes 24580
  95.1 106.3 %all-to-all-start = ((bf16[4,4,4,128,2,128]{5,2,1,0,4,3:T(4,128)(2,1)}), bf16[4,4,4,128,2,128]{5,2,1,0,4,3:T(4,128)(2,1)}, u32[]{:S(2)}, u32[]{:S(2)}) async-start(bf16[4,4,4,128,2,128]{5,2,1,0,4,3:T(4,128)(2,1)} %copy.69), calls=%async_computation | async-start | bytes 8388608 | tf_op jit(solution)/shard_map/all_to_all | solution.py:76
  201.5 4.7 %copy-start = (bf16[4,4,128,4,2,128]{5,4,3,2,1,0:T(2,128)(2,1)S(1)}, bf16[4,4,128,4,2,128]{5,4,3,2,1,0:T(2,128)(2,1)}, u32[]{:S(2)}) copy-start(bf16[4,4,128,4,2,128]{5,4,3,2,1,0:T(2,128)(2,1)} %param.10) | copy-start | bytes 12582916
  214.1 7.5 %copy-start.2 = (bf16[2,16,4]{1,2,0:T(4,128)(2,1)S(1)}, bf16[2,16,4]{1,2,0:T(4,128)(2,1)}, u32[]{:S(2)}) copy-start(bf16[2,16,4]{1,2,0:T(4,128)(2,1)} %param.7) | copy-start | bytes 772
  214.1 103.6 %all-to-all-start.1 = ((bf16[4,4,128,4,2,128]{5,3,1,0,4,2:T(4,128)(2,1)}), bf16[4,4,128,4,2,128]{5,3,1,0,4,2:T(4,128)(2,1)}, u32[]{:S(2)}, u32[]{:S(2)}) async-start(bf16[4,4,128,4,2,128]{5,3,1,0,4,2:T(4,128)(2,1)} %copy.75), calls=%async_computation.1 | async-start | bytes 8388608 | tf_op jit(solution)/shard_map/all_to_all | solution.py:84
  221.5 187.5 %reduce-scatter.2.cloned.1.call-start = ((), (), s32[]{:S(2)}) async-start(), calls=%async_computation.4 | async-start | bytes 4718592 | tf_op jit(solution)/shard_map/reduce_scatter | solution.py:97
Sparse Core Ops, SparseCore 0:
  9.1 58.9 all-gather.1
  357.2 51.7 reduce-scatter.1
where the time goes:
time: 419 us; the launch traced here: 418 us
  waiting for transfers between devices  298 us (71%)
  local copies, waits for them, and re-layouts  32.4 us (8%)
  matrix products  29.8 us (7%)
  other arithmetic  27.2 us (6%)
  starting transfers between devices  17.7 us (4%)
  between operations  13.6 us (3%)
    all_to_all x1, waiting for transfers between devices, shards(): lax.all_to_all(row_pass, 'space', split_axis=3, concat_axis=2, tiled=True)  96.1 us
    all_to_all x1, waiting for transfers between devices, shards(): lax.all_to_all(back_first, 'space', split_axis=2, concat_axis=3, tiled=True)  96.1 us
    all_gather x1, waiting for transfers between devices, shards(): lax.all_gather(spatial_coef, 'coil', axis=0, tiled=True)  53.7 us
    reduce_scatter x1, waiting for transfers between devices, shards(): lax.psum_scatter(jnp.einsum('txypz,tplq->lxyqz', combined, adjoint_mix(se...  51.9 us
    dot_general x4, matrix products, transform(): return jnp.einsum(form, volume, table, preferred_element_type=jnp.float32)  17.2 us
    all_to_all x1, starting transfers between devices, shards(): lax.all_to_all(row_pass, 'space', split_axis=3, concat_axis=2, tiled=True)  10.2 us
    add x1, other arithmetic, shards(): combined_real = cosine * sum_real + sine * sum_imaginary  9.64 us
  transfers between devices with their start and end apart: 4, of which 4 were waited for; matrix products, arithmetic and copies ran while one was open for 1% of the time, Pallas kernels for 0%

commit v1 on v0

--- a/solution.py
+++ b/solution.py
@@ -51,7 +51,9 @@
     section = temporal_basis
     image = jnp.einsum(
         "lxypz,lptq->txyqz",
-        lax.all_gather(spatial_coef, "coil", axis=0, tiled=True),
+        jnp.concatenate(
+            lax.all_to_all(jnp.stack([spatial_coef] * lax.axis_size("coil")), "coil", 0, 0), axis=0
+        ),
         forward_mix(section),
         preferred_element_type=jnp.float32,
     )

time: 419 us -> 442 us (1.055)
  local copies, waits for them, and re-layouts: 32.4 us -> 42.7 us
  starting transfers between devices: 17.7 us -> 26 us
    all_gather x1 -> x0, waiting for transfers between devices: 53.7 us -> none  [shards(): lax.all_gather(spatial_coef, 'coil', axis=0, tiled=True)]
    all_to_all x0 -> x1, waiting for transfers between devices: none -> 44.4 us  [shards(): lax.all_to_all(jnp.stack([spatial_coef] * lax.axis_size('coil')), 'coil',...]
    reduce_scatter x1, waiting for transfers between devices: 51.9 us -> 65.9 us  [shards(): lax.psum_scatter(jnp.einsum('txypz,tplq->lxyqz', combined, adjoint_mix(se...]
    all_to_all x0 -> x1, starting transfers between devices: none -> 6.34 us  [shards(): lax.all_to_all(jnp.stack([spatial_coef] * lax.axis_size('coil')), 'coil',...]
    another operation x0 -> x1, local copies, waits for them, and re-layouts: none -> 5.76 us  [shards(): jnp.stack([spatial_coef] * lax.axis_size('coil'))]
    all_to_all x0 -> x1, local copies, waits for them, and re-layouts: none -> 5.29 us  [shards(): lax.all_to_all(jnp.stack([spatial_coef] * lax.axis_size('coil')), 'coil',...]
where the time goes in v1:
time: 442 us; the launch traced here: 438 us
  waiting for transfers between devices  302 us (68%)
  local copies, waits for them, and re-layouts  42.7 us (10%)
  other arithmetic  27.5 us (6%)
  starting transfers between devices  26 us (6%)
  matrix products  25.7 us (6%)
  between operations  13.9 us (3%)
    all_to_all x1, waiting for transfers between devices, shards(): lax.all_to_all(back_first, 'space', split_axis=2, concat_axis=3, tiled=True)  96.1 us
    all_to_all x1, waiting for transfers between devices, shards(): lax.all_to_all(row_pass, 'space', split_axis=3, concat_axis=2, tiled=True)  96 us
    reduce_scatter x1, waiting for transfers between devices, shards(): lax.psum_scatter(jnp.einsum('txypz,tplq->lxyqz', combined, adjoint_mix(se...  65.9 us
    all_to_all x1, waiting for transfers between devices, shards(): lax.all_to_all(jnp.stack([spatial_coef] * lax.axis_size('coil')), 'coil',...  44.4 us
    dot_general x4, matrix products, transform(): return jnp.einsum(form, volume, table, preferred_element_type=jnp.float32)  17.2 us
    all_to_all x1, starting transfers between devices, shards(): lax.all_to_all(row_pass, 'space', split_axis=3, concat_axis=2, tiled=True)  12.3 us
    add x1, other arithmetic, shards(): combined_real = cosine * sum_real + sine * sum_imaginary  9.64 us
  transfers between devices with their start and end apart: 4, of which 4 were waited for; matrix products, arithmetic and copies ran while one was open for 1% of the time, Pallas kernels for 0%

profile of v1, /device:TPU:1, one launch (start us, length us, event | category | flops | bytes accessed | tf_op | source)
XLA Modules:
  0.0 438.0 jit_solution(8924631036186541403)
XLA Ops:
  6.5 1.9 copy.65
  8.4 5.8 %stack.170 = bf16[8,2,4,128,2,128]{5,1,4,3,2,0:T(2,128)(2,1)} broadcast(bf16[2,4,128,2,128]{4,0,3,2,1:T(2,128)(2,1)S(1)} %copy.65), dimensions={1,2,3,4,5} | broadcast | bytes 4718592 | tf_op jit(solution)/shard_map/stack | solution.py:55
  14.2 0.0 copy-start.4
  14.2 6.3 %all-to-all-start = ((bf16[8,2,4,128,2,128]{5,1,4,3,2,0:T(2,128)(2,1)}), bf16[8,2,4,128,2,128]{5,1,4,3,2,0:T(2,128)(2,1)}, u32[]{:S(2)}, u32[]{:S(2)}) async-start(bf16[8,2,4,128,2,128]{5,1,4,3,2,0:T(2,128)(2,1)} %stack.170), calls=%async_computation | async-start | bytes 8388608 | tf_op jit(solution)/shard_map/all_to_all | solution.py:55
  20.5 0.0 copy-done.4
  20.6 0.3 multiply_convert_fusion.2
  20.8 0.3 negate_convert_fusion
  21.1 0.3 multiply_convert_fusion
  21.4 0.7 fusion.47
  22.1 3.6 slice_convert_fusion.1
  25.7 44.4 %all-to-all-done = bf16[8,2,4,128,2,128]{5,1,4,3,2,0:T(2,128)(2,1)} async-done(((bf16[8,2,4,128,2,128]{5,1,4,3,2,0:T(2,128)(2,1)}), bf16[8,2,4,128,2,128]{5,1,4,3,2,0:T(2,128)(2,1)}, u32[]{:S(2)}, u32[]{:S(2)}) %all-to-all-start) | async-done | bytes 4194336 | tf_op jit(solution)/shard_map/all_to_all | solution.py:55
  70.1 5.3 %copy.66 = bf16[8,2,4,128,2,128]{5,1,0,4,3,2:T(2,128)(2,1)S(1)} copy(bf16[8,2,4,128,2,128]{5,1,4,3,2,0:T(2,128)(2,1)} %all-to-all-done) | data formatting | bytes 8388608 | tf_op jit(solution)/shard_map/all_to_all | solution.py:55
  75.4 0.0 copy-start.1
  75.4 0.7 convolution_bitcast_fusion
  76.2 0.3 copy.128
  76.4 0.0 copy-done.1
  76.4 5.0 %multiply_subtract_fusion = (f32[4,4,128,128]{3,2,1,0:T(8,128)S(1)}, f32[4,4,128,128]{3,2,1,0:T(8,128)S(1)}) fusion(f32[4,4,128,2,128]{4,2,1,0,3:T(8,128)S(1)} %bitcast.244, s32[4]{0:T(128)S(1)} %iota_add_fusion, s32[4,128,128]{2,1,0:T(8,128)S(1)} %copy-done.1), kind=kLoop, calls=%fused_computation.61 | loop fusion | flops 5242880 | bytes 4456464 | tf_op jit(solution)/shard_map/sub | solution.py:63
  81.4 0.0 copy-start.2
  81.4 0.0 copy-start.3
  81.4 3.1 subtract_convert_fusion
  84.6 0.0 copy-done.2
  84.6 0.0 copy-done.3
  84.6 6.7 %fusion.5 = bf16[4,4,4,128,2,128]{5,3,2,1,0,4:T(8,128)(2,1)} fusion(bf16[4,4,4,128,1,128]{5,3,4,2,1,0:T(8,128)(2,1)} %get-tuple-element.8, bf16[4,4,4,128,1,128]{5,3,4,2,1,0:T(8,128)(2,1)} %get-tuple-element.7, bf16[1,128,2,128]{3,1,0,2:T(8,128)(2,1)S(1)} %copy-done.2, bf16[1,128,2,128]{3,1,0,2:T(8,128)(2,1)S(1)} %copy-done.3), kind=kOutput, calls=%fused_computation.10 | convolution fusion | flops 2160590848 | bytes 8519680 | tf_op jit(solution)/shard_map/ctxypz,pyqk->ctxkqz/dot_general | solution.py:46
  91.3 7.4 %copy.69 = bf16[4,4,4,128,2,128]{5,2,1,0,4,3:T(4,128)(2,1)} copy(bf16[4,4,4,128,2,128]{5,3,2,1,0,4:T(8,128)(2,1)} %fusion.5) | data formatting | bytes 8388608 | tf_op jit(solution)/shard_map/convert_element_type | solution.py:75
  98.7 0.0 copy-start.5
  98.7 12.3 %all-to-all-start.1 = ((bf16[4,4,4,128,2,128]{5,2,1,0,4,3:T(4,128)(2,1)}), bf16[4,4,4,128,2,128]{5,2,1,0,4,3:T(4,128)(2,1)}, u32[]{:S(2)}, u32[]{:S(2)}) async-start(bf16[4,4,4,128,2,128]{5,2,1,0,4,3:T(4,128)(2,1)} %copy.69), calls=%async_computation.1 | async-start | bytes 8388608 | tf_op jit(solution)/shard_map/all_to_all | solution.py:78
  111.0 0.0 copy-done.5
  111.1 96.0 %all-to-all-done.1 = bf16[4,4,4,128,2,128]{5,2,1,0,4,3:T(4,128)(2,1)} async-done(((bf16[4,4,4,128,2,128]{5,2,1,0,4,3:T(4,128)(2,1)}), bf16[4,4,4,128,2,128]{5,2,1,0,4,3:T(4,128)(2,1)}, u32[]{:S(2)}, u32[]{:S(2)}) %all-to-all-start.1) | async-done | bytes 4194336 | tf_op jit(solution)/shard_map/all_to_all | solution.py:78
  207.0 0.0 copy-start
  207.0 4.7 %copy.70 = bf16[4,4,4,32,4,2,128]{6,2,3,5,4,1,0:T(4,128)(2,1)S(1)} copy(bf16[4,4,4,32,4,2,128]{6,2,1,0,5,4,3:T(4,128)(2,1)} %bitcast.52) | data formatting | bytes 8388608 | tf_op jit(solution)/shard_map/all_to_all | solution.py:78
  211.7 0.0 copy-done
  211.8 1.4 fusion.1
  213.1 1.3 fusion.6
  214.4 5.2 %copy.75 = bf16[4,4,128,4,2,128]{5,3,1,0,4,2:T(4,128)(2,1)} copy(bf16[4,4,128,4,2,128]{5,2,3,1,0,4:T(8,128)(2,1)S(1)} %fusion.6) | data formatting | bytes 8388608 | tf_op jit(solution)/shard_map/convert_element_type | solution.py:83
  219.7 7.3 %all-to-all-start.2 = ((bf16[4,4,128,4,2,128]{5,3,1,0,4,2:T(4,128)(2,1)}), bf16[4,4,128,4,2,128]{5,3,1,0,4,2:T(4,128)(2,1)}, u32[]{:S(2)}, u32[]{:S(2)}) async-start(bf16[4,4,128,4,2,128]{5,3,1,0,4,2:T(4,128)(2,1)} %copy.75), calls=%async_computation.2 | async-start | bytes 8388608 | tf_op jit(solution)/shard_map/all_to_all | solution.py:86
  226.9 0.0 reduce-scatter.2.cloned.1.call-start
  227.0 96.1 %all-to-all-done.2 = bf16[4,4,128,4,2,128]{5,3,1,0,4,2:T(4,128)(2,1)} async-done(((bf16[4,4,128,4,2,128]{5,3,1,0,4,2:T(4,128)(2,1)}), bf16[4,4,128,4,2,128]{5,3,1,0,4,2:T(4,128)(2,1)}, u32[]{:S(2)}, u32[]{:S(2)}) %all-to-all-start.2) | async-done | bytes 4194336 | tf_op jit(solution)/shard_map/all_to_all | solution.py:86
  323.1 6.5 %copy.76 = bf16[4,4,32,4,4,2,128]{6,4,2,5,3,1,0:T(4,128)(2,1)} copy(bf16[4,4,32,4,4,2,128]{6,4,1,0,5,3,2:T(4,128)(2,1)} %bitcast.63) | data formatting | bytes 8388608 | tf_op jit(solution)/shard_map/all_to_all | solution.py:86
  329.6 7.8 %fusion.17 = f32[4,4,4,128,2,128]{5,3,4,2,1,0:T(8,128)} fusion(bf16[4,4,4,128,2,128,1]{5,3,6,4,2,1,0:T(8,128)(2,1)} %bitcast.237, bf16[1,128,2,128]{3,1,2,0:T(8,128)(2,1)S(1)} %get-tuple-element.18, bf16[1,128,2,128]{3,1,2,0:T(8,128)(2,1)S(1)} %get-tuple-element.15), kind=kOutput, calls=%fused_computation.28 | convolution fusion | flops 2150105088 | bytes 12713984 | tf_op jit(solution)/shard_map/ctxypz,pzqk->ctxyqk/dot_general | solution.py:46
  337.4 4.6 %add_reduce_fusion = (f32[4,4,128,128]{3,2,1,0:T(8,128)S(1)}, f32[4,4,128,128]{3,2,1,0:T(8,128)S(1)}) fusion(f32[4,4,4,128,2,128]{5,3,4,2,1,0:T(8,128)} %fusion.17, f32[4,4,128,128]{3,2,1,0:T(8,128)S(1)} %bitcast.243, f32[4,4,128,128]{3,2,1,0:T(8,128)S(1)} %bitcast.241), kind=kLoop, calls=%fused_computation.25 | loop fusion | flops 7864320 | bytes 12582912 | tf_op jit(solution)/shard_map/reduce_sum | solution.py:93
  342.0 9.6 %fusion.34 = (f32[4,4,128,1,128]{4,0,3,2,1:T(4,128)S(1)}, f32[4,4,128,1,128]{4,0,3,2,1:T(4,128)S(1)}) fusion(f32[4,4,128,128]{3,2,1,0:T(8,128)S(1)} %get-tuple-element.6, f32[4,4,128,128]{3,2,1,0:T(8,128)S(1)} %get-tuple-element.5, s32[4]{0:T(128)S(1)} %iota_add_fusion, s32[4,128,128]{2,1,0:T(8,128)S(1)} %copy-done.1), kind=kLoop, calls=%fused_computation.55 | loop fusion | flops 5242880 | bytes 4456464 | tf_op jit(solution)/shard_map/add | solution.py:95
  351.6 7.8 %fusion.7 = bf16[16,4,128,2,128]{4,0,2,1,3:T(8,128)(2,1)S(1)} fusion(f32[4,4,128,1,128]{4,0,3,2,1:T(4,128)S(1)} %get-tuple-element.10, f32[4,4,128,1,128]{4,0,3,2,1:T(4,128)S(1)} %get-tuple-element.9, f32[4,1,16,2]{2,0,1,3:T(4,128)S(1)} %get-tuple-element.22, f32[4,1,16,2]{2,0,1,3:T(4,128)S(1)} %get-tuple-element.21), kind=kOutput, calls=%fused_computation.12 | convolution fusion | flops 203948288 | bytes 6292480 | tf_op jit(solution)/shard_map/txypz,tplq->lxyqz/dot_general | solution.py:100
  359.4 3.1 copy.82
  362.4 0.0 reduce-scatter.2.cloned.1.call-update
  362.5 65.9 %reduce-scatter.2.cloned.1.call-done = bf16[2,4,128,2,128]{4,2,3,1,0:T(8,128)(2,1)} async-done(((bf16[16,4,128,2,128]{4,2,3,1,0:T(8,128)(2,1)}), bf16[2,4,128,2,128]{4,2,3,1,0:T(8,128)(2,1)}) %reduce-scatter.2.cloned.1.call-update) | async-done | bytes 524304 | tf_op jit(solution)/shard_map/reduce_scatter | solution.py:99
  428.4 2.6 copy.83
  (9 shorter events, 0.0 us)
Async XLA Ops:
  14.2 6.4 %copy-start.4 = (bf16[2,16,4]{1,2,0:T(4,128)(2,1)S(1)}, bf16[2,16,4]{1,2,0:T(4,128)(2,1)}, u32[]{:S(2)}) copy-start(bf16[2,16,4]{1,2,0:T(4,128)(2,1)} %param.7) | copy-start | bytes 772
  14.2 56.0 %all-to-all-start = ((bf16[8,2,4,128,2,128]{5,1,4,3,2,0:T(2,128)(2,1)}), bf16[8,2,4,128,2,128]{5,1,4,3,2,0:T(2,128)(2,1)}, u32[]{:S(2)}, u32[]{:S(2)}) async-start(bf16[8,2,4,128,2,128]{5,1,4,3,2,0:T(2,128)(2,1)} %stack.170), calls=%async_computation | async-start | bytes 8388608 | tf_op jit(solution)/shard_map/all_to_all | solution.py:55
  75.4 1.0 copy-start.1
  81.4 3.2 copy-start.2
  81.4 3.1 copy-start.3
  98.7 12.3 %copy-start.5 = (s32[4,4,128]{2,1,0:T(4,128)S(1)}, s32[4,4,128]{2,1,0:T(4,128)}, u32[]{:S(2)}) copy-start(s32[4,4,128]{2,1,0:T(4,128)} %param.11) | copy-start | bytes 24580
  98.7 108.3 %all-to-all-start.1 = ((bf16[4,4,4,128,2,128]{5,2,1,0,4,3:T(4,128)(2,1)}), bf16[4,4,4,128,2,128]{5,2,1,0,4,3:T(4,128)(2,1)}, u32[]{:S(2)}, u32[]{:S(2)}) async-start(bf16[4,4,4,128,2,128]{5,2,1,0,4,3:T(4,128)(2,1)} %copy.69), calls=%async_computation.1 | async-start | bytes 8388608 | tf_op jit(solution)/shard_map/all_to_all | solution.py:78
  207.0 4.7 %copy-start = (bf16[4,4,128,4,2,128]{5,4,3,2,1,0:T(2,128)(2,1)S(1)}, bf16[4,4,128,4,2,128]{5,4,3,2,1,0:T(2,128)(2,1)}, u32[]{:S(2)}) copy-start(bf16[4,4,128,4,2,128]{5,4,3,2,1,0:T(2,128)(2,1)} %param.10) | copy-start | bytes 12582916
  219.7 103.4 %all-to-all-start.2 = ((bf16[4,4,128,4,2,128]{5,3,1,0,4,2:T(4,128)(2,1)}), bf16[4,4,128,4,2,128]{5,3,1,0,4,2:T(4,128)(2,1)}, u32[]{:S(2)}, u32[]{:S(2)}) async-start(bf16[4,4,128,4,2,128]{5,3,1,0,4,2:T(4,128)(2,1)} %copy.75), calls=%async_computation.2 | async-start | bytes 8388608 | tf_op jit(solution)/shard_map/all_to_all | solution.py:86
  226.9 201.5 %reduce-scatter.2.cloned.1.call-start = ((), (), s32[]{:S(2)}) async-start(), calls=%async_computation.4 | async-start | bytes 4718592 | tf_op jit(solution)/shard_map/reduce_scatter | solution.py:99
Sparse Core Ops, SparseCore 0:
  362.6 65.7 reduce-scatter.1
